TPU v7x, 32 devices: a whole 2x2x4 slice. The times are simulated.
32 devices in a mesh: ctx: 8 (over z, x), tp: 4 (over y, core).
Axes of the slice: x: 2, y: 2, z: 4, core: 2. Of those that a mesh axis runs over, the one named last changes fastest.
Arguments:
- q_raw: bfloat16 [2048, 4096], P('ctx', 'tp'), may hold values from -36 to 36
- k_raw: bfloat16 [2048, 2048], P('ctx', 'tp'), may hold values from -36 to 36
- v_cur: bfloat16 [2048, 2048], P('ctx', 'tp'), may hold values from -6 to 6
- d_out: bfloat16 [2048, 4096], P('ctx', 'tp'), may hold values from -6 to 6
- q_gain: float32 [128], replicated, may hold values from 0.25 to 1.75
- k_gain: float32 [128], replicated, may hold values from 0.25 to 1.75
Outputs:
- dq_raw: bfloat16 [2048, 4096], P('ctx', 'tp')
- dk_raw: bfloat16 [2048, 2048], P('ctx', 'tp')
- dv: bfloat16 [2048, 2048], P('ctx', 'tp')
- q_gain_grad: float32 [128], replicated
- k_gain_grad: float32 [128], replicated
All inputs are finite; a program needn't handle non-finite values.
Results may differ from a plain program's by a relative error of at most 0.0077.
Values may be sent and summed in bfloat16 or wider, within the bound.
A program may use at most 64 MiB of HBM per device.

v0:
```python
import jax
import jax.numpy as jnp
from jax import lax
from jax.sharding import PartitionSpec as P

Q_HEADS = 32
KV_HEADS = 16
HEAD_DIM = 128
WINDOW = 1024


score_scale = 168.0 ** (-0.5)
epsilon = 1e-06


def shifted(value, axis, by):
    devices = lax.axis_size(axis)
    pairs = [(i, i + by) for i in range(devices) if 0 <= i + by < devices]
    return lax.ppermute(value, axis, pairs)


def normalize(raw32, gain):
    vectors = raw32.reshape(raw32.shape[0], -1, HEAD_DIM)
    inverse = lax.rsqrt(jnp.mean(vectors * vectors, axis=-1, keepdims=True) + epsilon)
    return vectors * inverse * gain


def per_device(q_raw, k_raw, v_cur, d_out, q_gain, k_gain):
    row_count = q_raw.shape[0]
    hop_count = WINDOW // row_count
    q_normed, pull_query = jax.vjp(normalize, q_raw.astype(jnp.float32), q_gain)
    k_normed, pull_key = jax.vjp(normalize, k_raw.astype(jnp.float32), k_gain)
    q_low = q_normed.astype(jnp.bfloat16)
    k_low = k_normed.astype(jnp.bfloat16)
    local_kv = k_low.shape[1]
    local_q = q_low.shape[1]
    group = local_q // local_kv
    value_low = v_cur.reshape(row_count, local_kv, HEAD_DIM)
    grad_out = d_out.reshape(row_count, local_q, HEAD_DIM)
    earlier = []
    for distance in range(1, hop_count + 1):
        earlier.append(shifted((k_low, value_low), "ctx", distance))
    band_keys = jnp.concatenate(
        [earlier[d][0] for d in reversed(range(hop_count))] + [k_low], axis=0
    )
    band_values = jnp.concatenate(
        [earlier[d][1] for d in reversed(range(hop_count))] + [value_low], axis=0
    )
    band_width = (hop_count + 1) * row_count
    device_index = lax.axis_index("ctx")
    row_ids = lax.broadcasted_iota(jnp.int32, (row_count, band_width), 0)
    col_ids = lax.broadcasted_iota(jnp.int32, (row_count, band_width), 1)
    distance_ids = row_ids + hop_count * row_count - col_ids
    band_start = (device_index - hop_count) * row_count
    visible = (distance_ids >= 0) & (distance_ids < WINDOW) & (band_start + col_ids >= 0)
    dq_parts = []
    dk_parts = []
    dv_parts = []
    for kv_head in range(local_kv):
        queries = q_low[:, kv_head * group : (kv_head + 1) * group]
        grads = grad_out[:, kv_head * group : (kv_head + 1) * group]
        head_keys = band_keys[:, kv_head]
        head_values = band_values[:, kv_head]
        scores = (
            jnp.einsum("tgd,cd->gtc", queries, head_keys, preferred_element_type=jnp.float32)
            * score_scale
        )
        exp_scores = jnp.where(visible, jnp.exp(scores), 0.0)
        probs = exp_scores / jnp.sum(exp_scores, axis=-1, keepdims=True)
        dprobs = jnp.einsum("tgd,cd->gtc", grads, head_values, preferred_element_type=jnp.float32)
        row_delta = jnp.sum(probs * dprobs, axis=-1, keepdims=True)
        dscores = (probs * (dprobs - row_delta) * score_scale).astype(jnp.bfloat16)
        probs_low = probs.astype(jnp.bfloat16)
        dq_parts.append(
            jnp.einsum("gtc,cd->tgd", dscores, head_keys, preferred_element_type=jnp.float32)
        )
        dk_parts.append(
            jnp.einsum("gtc,tgd->cd", dscores, queries, preferred_element_type=jnp.float32).astype(
                jnp.bfloat16
            )
        )
        dv_parts.append(
            jnp.einsum("gtc,tgd->cd", probs_low, grads, preferred_element_type=jnp.float32).astype(
                jnp.bfloat16
            )
        )
    query_grad = jnp.concatenate(dq_parts, axis=1)
    key_blocks = jnp.stack(dk_parts, axis=1).reshape(hop_count + 1, row_count, local_kv, HEAD_DIM)
    value_blocks = jnp.stack(dv_parts, axis=1).reshape(hop_count + 1, row_count, local_kv, HEAD_DIM)
    key_grad = key_blocks[hop_count].astype(jnp.float32)
    value_grad = value_blocks[hop_count].astype(jnp.float32)
    for distance in range(1, hop_count + 1):
        got_key, got_value = shifted(
            (key_blocks[hop_count - distance], value_blocks[hop_count - distance]), "ctx", -distance
        )
        key_grad = key_grad + got_key.astype(jnp.float32)
        value_grad = value_grad + got_value.astype(jnp.float32)
    dq_raw32, q_gain_part = pull_query(query_grad)
    dk_raw32, k_gain_part = pull_key(key_grad)
    gain_totals = lax.psum((q_gain_part, k_gain_part), ("ctx", "tp"))
    token_total = row_count * lax.axis_size("ctx")
    q_gain_grad = gain_totals[0] / jnp.sqrt(jnp.float32(token_total * Q_HEADS))
    k_gain_grad = gain_totals[1] / jnp.sqrt(jnp.float32(token_total * KV_HEADS))
    dq_raw = dq_raw32.astype(jnp.bfloat16)
    dk_raw = dk_raw32.astype(jnp.bfloat16)
    dv = value_grad.reshape(row_count, -1).astype(jnp.bfloat16)
    return (dq_raw, dk_raw, dv, q_gain_grad, k_gain_grad)


def solution(mesh):
    return jax.shard_map(
        per_device,
        mesh=mesh,
        in_specs=(P("ctx", "tp"), P("ctx", "tp"), P("ctx", "tp"), P("ctx", "tp"), P(), P()),
        out_specs=(P("ctx", "tp"), P("ctx", "tp"), P("ctx", "tp"), P(), P()),
        check_vma=False,
    )
```

profile of v0, /device:TPU:0, one launch (start us, length us, event | category | flops | bytes accessed | tf_op | source)
XLA Modules:
  0.0 263.9 jit_solution(4225913662095262754)
XLA Ops:
  2.0 5.5 %collective-permute-start.7 = (bf16[256,4,128]{2,0,1:T(8,128)(2,1)S(1)}, bf16[256,4,128]{2,0,1:T(8,128)(2,1)}, u32[]{:S(2)}, u32[]{:S(2)}) collective-permute-start(bf16[256,4,128]{2,0,1:T(8,128)(2,1)S(1)} %copy.106), channel_id=1, source_target_pairs={{0,4},{4,8},{8,12},{12,16},{16,20},{20,24},{24,28},{1,5},{5,9},{9,... | collective-permute-start | bytes 786440 | tf_op jit(solution)/shard_map/ppermute | solution.py:19
  7.5 3.5 %collective-permute-start.6 = (bf16[256,4,128]{2,0,1:T(8,128)(2,1)S(1)}, bf16[256,4,128]{2,0,1:T(8,128)(2,1)}, u32[]{:S(2)}, u32[]{:S(2)}) collective-permute-start(bf16[256,4,128]{2,0,1:T(8,128)(2,1)S(1)} %copy.106), channel_id=1, source_target_pairs={{0,8},{4,12},{8,16},{12,20},{16,24},{20,28},{1,9},{5,13},{9,17},{1... | collective-permute-start | bytes 786440 | tf_op jit(solution)/shard_map/ppermute | solution.py:19
  13.3 3.6 %collective-permute-start.2 = (bf16[256,4,128]{2,0,1:T(8,128)(2,1)}, bf16[256,4,128]{2,0,1:T(8,128)(2,1)}, u32[]{:S(2)}, u32[]{:S(2)}) collective-permute-start(bf16[256,4,128]{2,0,1:T(8,128)(2,1)} %multiply_convert_fusion.1), channel_id=1, source_target_pairs={{0,8},{4,12},{8,16},{12,20},{16,24},{20,28},{1,9},{5,13},{9,17},{1... | collective-permute-start | bytes 786440 | tf_op jit(solution)/shard_map/ppermute | solution.py:19
  24.8 8.0 %collective-permute-done = bf16[256,4,128]{2,0,1:T(8,128)(2,1)} collective-permute-done((bf16[256,4,128]{2,0,1:T(8,128)(2,1)}, bf16[256,4,128]{2,0,1:T(8,128)(2,1)}, u32[]{:S(2)}, u32[]{:S(2)}) %collective-permute-start) | collective-permute-done | bytes 262176 | tf_op jit(solution)/shard_map/ppermute | solution.py:19
  32.8 5.7 %collective-permute-start.3 = (bf16[256,4,128]{2,0,1:T(8,128)(2,1)}, bf16[256,4,128]{2,0,1:T(8,128)(2,1)S(1)}, u32[]{:S(2)}, u32[]{:S(2)}) collective-permute-start(bf16[256,4,128]{2,0,1:T(8,128)(2,1)} %multiply_convert_fusion.1), channel_id=1, source_target_pairs={{0,4},{4,8},{8,12},{12,16},{16,20},{20,24},{24,28},{1,5},{5,9},{9,... | collective-permute-start | bytes 786440 | tf_op jit(solution)/shard_map/ppermute | solution.py:19
  40.2 16.8 %collective-permute-start.5 = (bf16[256,4,128]{2,0,1:T(8,128)(2,1)S(1)}, bf16[256,4,128]{2,0,1:T(8,128)(2,1)}, u32[]{:S(2)}, u32[]{:S(2)}) collective-permute-start(bf16[256,4,128]{2,0,1:T(8,128)(2,1)S(1)} %copy.106), channel_id=1, source_target_pairs={{0,12},{4,16},{8,20},{12,24},{16,28},{1,13},{5,17},{9,21},{13,25},... | collective-permute-start | bytes 786440 | tf_op jit(solution)/shard_map/ppermute | solution.py:19
  58.6 14.0 %collective-permute-start.4 = (bf16[256,4,128]{2,0,1:T(8,128)(2,1)S(1)}, bf16[256,4,128]{2,0,1:T(8,128)(2,1)}, u32[]{:S(2)}, u32[]{:S(2)}) collective-permute-start(bf16[256,4,128]{2,0,1:T(8,128)(2,1)S(1)} %copy.106), channel_id=1, source_target_pairs={{0,16},{4,20},{8,24},{12,28},{1,17},{5,21},{9,25},{13,29},{2,18},{... | collective-permute-start | bytes 786440 | tf_op jit(solution)/shard_map/ppermute | solution.py:19
  76.1 3.5 %fusion.77 = f32[2,256,1280]{1,2,0:T(8,128)} fusion(pred[256,1280]{0,1:T(8,128)(4,1)} %fusion.95, bf16[1280,4,128]{2,0,1:T(8,128)(2,1)} %constant_dynamic-update-slice_fusion, bf16[256,8,128]{2,0,1:T(8,128)(2,1)S(1)} %copy-done.7), kind=kOutput, calls=%fused_computation.86 | convolution fusion | flops 169740032 | bytes 3407872 | tf_op jit(solution)/shard_map/div | solution.py:69
  79.6 3.5 %fusion.79 = f32[2,256,1280]{1,2,0:T(8,128)} fusion(pred[256,1280]{0,1:T(8,128)(4,1)} %fusion.95, bf16[1280,4,128]{2,0,1:T(8,128)(2,1)} %constant_dynamic-update-slice_fusion, bf16[256,8,128]{2,0,1:T(8,128)(2,1)S(1)} %copy-done.7), kind=kOutput, calls=%fused_computation.88 | convolution fusion | flops 169740032 | bytes 3407872 | tf_op jit(solution)/shard_map/div | solution.py:69
  83.0 3.5 %fusion.81 = f32[2,256,1280]{1,2,0:T(8,128)} fusion(pred[256,1280]{0,1:T(8,128)(4,1)} %fusion.95, bf16[1280,4,128]{2,0,1:T(8,128)(2,1)} %constant_dynamic-update-slice_fusion, bf16[256,8,128]{2,0,1:T(8,128)(2,1)S(1)} %copy-done.7), kind=kOutput, calls=%fused_computation.90 | convolution fusion | flops 169740032 | bytes 3407872 | tf_op jit(solution)/shard_map/div | solution.py:69
  86.5 3.5 %fusion.91 = f32[2,256,1280]{1,2,0:T(8,128)} fusion(pred[256,1280]{0,1:T(8,128)(4,1)} %fusion.95, bf16[1280,4,128]{2,0,1:T(8,128)(2,1)} %constant_dynamic-update-slice_fusion, bf16[256,8,128]{2,0,1:T(8,128)(2,1)S(1)} %copy-done.7), kind=kOutput, calls=%fused_computation.100 | convolution fusion | flops 169740032 | bytes 3407872 | tf_op jit(solution)/shard_map/div | solution.py:69
  97.5 5.8 %fusion.96 = f32[256,2,128]{2,0,1:T(8,128)} fusion(f32[2,256,1280]{1,2,0:T(8,128)} %fusion.77, f32[2,256,1280]{1,2,0:T(8,128)} %convolution_bitcast_fusion, bf16[1280,4,128]{2,0,1:T(8,128)(2,1)} %constant_dynamic-update-slice_fusion), kind=kOutput, calls=%fused_computation.106 | convolution fusion | flops 171050752 | bytes 11075584 | tf_op jit(solution)/shard_map/gtc,cd->tgd/dot_general | solution.py:75
  103.3 5.6 %fusion.48 = bf16[1280,1,128]{2,0,1:T(8,128)(2,1)} fusion(f32[2,256,1280]{1,2,0:T(8,128)} %fusion.77, f32[2,256,1280]{1,2,0:T(8,128)} %convolution_bitcast_fusion, bf16[256,8,128]{2,0,1:T(8,128)(2,1)S(1)} %copy-done.7), kind=kOutput, calls=%fused_computation.68 | convolution fusion | flops 171214592 | bytes 10944512 | tf_op jit(solution)/shard_map/gtc,tgd->cd/dot_general | solution.py:78
  108.9 3.2 %convolution_bitcast_fusion.1 = f32[2,256,1280]{1,2,0:T(8,128)} fusion(bf16[1280,4,128]{2,0,1:T(8,128)(2,1)} %copy-done.4, bf16[256,8,128]{0,2,1:T(8,128)(2,1)S(1)} %bitcast.191), kind=kOutput, calls=%fused_computation.21 | convolution fusion | flops 167772160 | bytes 3080192 | tf_op jit(solution)/shard_map/tgd,cd->gtc/dot_general | solution.py:70
  113.3 5.8 %fusion.99 = f32[256,2,128]{2,0,1:T(8,128)} fusion(f32[2,256,1280]{1,2,0:T(8,128)} %fusion.79, f32[2,256,1280]{1,2,0:T(8,128)} %convolution_bitcast_fusion.1, bf16[1280,4,128]{2,0,1:T(8,128)(2,1)} %constant_dynamic-update-slice_fusion), kind=kOutput, calls=%fused_computation.107 | convolution fusion | flops 171050752 | bytes 11075584 | tf_op jit(solution)/shard_map/gtc,cd->tgd/dot_general | solution.py:75
  119.1 5.6 %fusion.49 = bf16[1280,1,128]{2,0,1:T(8,128)(2,1)} fusion(f32[2,256,1280]{1,2,0:T(8,128)} %fusion.79, f32[2,256,1280]{1,2,0:T(8,128)} %convolution_bitcast_fusion.1, bf16[256,8,128]{2,0,1:T(8,128)(2,1)S(1)} %copy-done.7), kind=kOutput, calls=%fused_computation.69 | convolution fusion | flops 171214592 | bytes 10944512 | tf_op jit(solution)/shard_map/gtc,tgd->cd/dot_general | solution.py:78
  129.1 5.8 %fusion.102 = f32[256,2,128]{2,0,1:T(8,128)} fusion(f32[2,256,1280]{1,2,0:T(8,128)} %fusion.81, f32[2,256,1280]{1,2,0:T(8,128)} %convolution_bitcast_fusion.2, bf16[1280,4,128]{2,0,1:T(8,128)(2,1)} %constant_dynamic-update-slice_fusion), kind=kOutput, calls=%fused_computation.108 | convolution fusion | flops 171050752 | bytes 11075584 | tf_op jit(solution)/shard_map/gtc,cd->tgd/dot_general | solution.py:75
  134.9 5.6 %fusion.50 = bf16[1280,1,128]{2,0,1:T(8,128)(2,1)} fusion(f32[2,256,1280]{1,2,0:T(8,128)} %fusion.81, f32[2,256,1280]{1,2,0:T(8,128)} %convolution_bitcast_fusion.2, bf16[256,8,128]{2,0,1:T(8,128)(2,1)S(1)} %copy-done.7), kind=kOutput, calls=%fused_computation.70 | convolution fusion | flops 171214592 | bytes 10944512 | tf_op jit(solution)/shard_map/gtc,tgd->cd/dot_general | solution.py:78
  140.5 3.1 %convolution_bitcast_fusion.3 = f32[2,256,1280]{1,2,0:T(8,128)} fusion(bf16[1280,4,128]{2,0,1:T(8,128)(2,1)} %copy-done.4, bf16[256,8,128]{0,2,1:T(8,128)(2,1)S(1)} %bitcast.195), kind=kOutput, calls=%fused_computation.23 | convolution fusion | flops 167772160 | bytes 3080192 | tf_op jit(solution)/shard_map/tgd,cd->gtc/dot_general | solution.py:70
  144.9 6.0 %fusion.105 = f32[256,2,128]{2,0,1:T(8,128)} fusion(f32[2,256,1280]{1,2,0:T(8,128)} %fusion.91, f32[2,256,1280]{1,2,0:T(8,128)} %convolution_bitcast_fusion.3, bf16[1280,4,128]{2,0,1:T(8,128)(2,1)} %constant_dynamic-update-slice_fusion), kind=kOutput, calls=%fused_computation.109 | convolution fusion | flops 171050752 | bytes 11075584 | tf_op jit(solution)/shard_map/gtc,cd->tgd/dot_general | solution.py:75
  151.0 5.6 %fusion.51 = bf16[1280,1,128]{2,0,1:T(8,128)(2,1)} fusion(f32[2,256,1280]{1,2,0:T(8,128)} %fusion.91, f32[2,256,1280]{1,2,0:T(8,128)} %convolution_bitcast_fusion.3, bf16[256,8,128]{2,0,1:T(8,128)(2,1)S(1)} %copy-done.7), kind=kOutput, calls=%fused_computation.71 | convolution fusion | flops 171214592 | bytes 10944512 | tf_op jit(solution)/shard_map/gtc,tgd->cd/dot_general | solution.py:78
  175.4 12.9 %collective-permute-done.15 = bf16[256,4,128]{0,2,1:T(8,128)(2,1)} collective-permute-done((bf16[256,4,128]{0,2,1:T(8,128)(2,1)}, bf16[256,4,128]{0,2,1:T(8,128)(2,1)}, u32[]{:S(2)}, u32[]{:S(2)}) %collective-permute-start.15) | collective-permute-done | bytes 262176 | tf_op jit(solution)/shard_map/ppermute | solution.py:19
  193.1 23.3 %collective-permute-done.11 = bf16[256,4,128]{2,0,1:T(8,128)(2,1)} collective-permute-done((bf16[256,4,128]{2,0,1:T(8,128)(2,1)}, bf16[256,4,128]{2,0,1:T(8,128)(2,1)}, u32[]{:S(2)}, u32[]{:S(2)}) %collective-permute-start.11) | collective-permute-done | bytes 262176 | tf_op jit(solution)/shard_map/ppermute | solution.py:19
  219.3 44.1 %all-reduce = (f32[128]{0:T(128)S(1)}, f32[128]{0:T(128)S(1)}) all-reduce(f32[128]{0:T(128)S(1)} %bitcast_reduce_fusion, f32[128]{0:T(128)S(1)} %get-tuple-element.20), channel_id=1, replica_groups=mesh['ctx'=8,'tp'=4] {'ctx','tp'}, use_global_device_ids=true, to_apply=%region_14.15 | all-reduce | flops 256 | bytes 2048 | tf_op jit(solution)/shard_map/psum | solution.py:100
  (102 shorter events, 59.6 us)
Async XLA Ops:
  0.6 11.7 %copy-start.12 = (f32[128]{0:T(128)S(1)}, f32[128]{0:T(128)}, u32[]{:S(2)}) copy-start(f32[128]{0:T(128)} %param.11) | copy-start | bytes 1540
  0.6 21.1 %copy-start.5 = (bf16[256,1024]{1,0:T(8,128)(2,1)S(1)}, bf16[256,1024]{1,0:T(8,128)(2,1)}, u32[]{:S(2)}) copy-start(bf16[256,1024]{1,0:T(8,128)(2,1)} %param.6) | copy-start | bytes 1572868
  2.0 91.1 %collective-permute-start.7 = (bf16[256,4,128]{2,0,1:T(8,128)(2,1)S(1)}, bf16[256,4,128]{2,0,1:T(8,128)(2,1)}, u32[]{:S(2)}, u32[]{:S(2)}) collective-permute-start(bf16[256,4,128]{2,0,1:T(8,128)(2,1)S(1)} %copy.106), channel_id=1, source_target_pairs={{0,4},{4,8},{8,12},{12,16},{16,20},{20,24},{24,28},{1,5},{5,9},{9,... | collective-permute-start | bytes 786440 | tf_op jit(solution)/shard_map/ppermute | solution.py:19
  7.5 84.6 %collective-permute-start.6 = (bf16[256,4,128]{2,0,1:T(8,128)(2,1)S(1)}, bf16[256,4,128]{2,0,1:T(8,128)(2,1)}, u32[]{:S(2)}, u32[]{:S(2)}) collective-permute-start(bf16[256,4,128]{2,0,1:T(8,128)(2,1)S(1)} %copy.106), channel_id=1, source_target_pairs={{0,8},{4,12},{8,16},{12,20},{16,24},{20,28},{1,9},{5,13},{9,17},{1... | collective-permute-start | bytes 786440 | tf_op jit(solution)/shard_map/ppermute | solution.py:19
  12.1 11.3 %copy-start.13 = (f32[128]{0:T(128)S(1)}, f32[128]{0:T(128)}, u32[]{:S(2)}) copy-start(f32[128]{0:T(128)} %param.10) | copy-start | bytes 1540
  13.3 11.3 %copy-start.6 = (bf16[256,1024]{1,0:T(8,128)(2,1)S(1)}, bf16[256,1024]{1,0:T(8,128)(2,1)}, u32[]{:S(2)}) copy-start(bf16[256,1024]{1,0:T(8,128)(2,1)} %param.9) | copy-start | bytes 1572868
  13.3 45.4 %collective-permute-start.2 = (bf16[256,4,128]{2,0,1:T(8,128)(2,1)}, bf16[256,4,128]{2,0,1:T(8,128)(2,1)}, u32[]{:S(2)}, u32[]{:S(2)}) collective-permute-start(bf16[256,4,128]{2,0,1:T(8,128)(2,1)} %multiply_convert_fusion.1), channel_id=1, source_target_pairs={{0,8},{4,12},{8,16},{12,20},{16,24},{20,28},{1,9},{5,13},{9,17},{1... | collective-permute-start | bytes 786440 | tf_op jit(solution)/shard_map/ppermute | solution.py:19
  16.9 23.3 %collective-permute-start.1 = (bf16[256,4,128]{2,0,1:T(8,128)(2,1)}, bf16[256,4,128]{2,0,1:T(8,128)(2,1)}, u32[]{:S(2)}, u32[]{:S(2)}) collective-permute-start(bf16[256,4,128]{2,0,1:T(8,128)(2,1)} %multiply_convert_fusion.1), channel_id=1, source_target_pairs={{0,12},{4,16},{8,20},{12,24},{16,28},{1,13},{5,17},{9,21},{13,25},... | collective-permute-start | bytes 786440 | tf_op jit(solution)/shard_map/ppermute | solution.py:19
  19.8 13.0 %collective-permute-start = (bf16[256,4,128]{2,0,1:T(8,128)(2,1)}, bf16[256,4,128]{2,0,1:T(8,128)(2,1)}, u32[]{:S(2)}, u32[]{:S(2)}) collective-permute-start(bf16[256,4,128]{2,0,1:T(8,128)(2,1)} %multiply_convert_fusion.1), channel_id=1, source_target_pairs={{0,16},{4,20},{8,24},{12,28},{1,17},{5,21},{9,25},{13,29},{2,18},{... | collective-permute-start | bytes 786440 | tf_op jit(solution)/shard_map/ppermute | solution.py:19
  24.8 51.2 %copy-start.7 = (bf16[256,8,128]{2,0,1:T(8,128)(2,1)S(1)}, bf16[256,8,128]{2,0,1:T(8,128)(2,1)}, u32[]{:S(2)}) copy-start(bf16[256,8,128]{2,0,1:T(8,128)(2,1)} %multiply_convert_fusion) | copy-start | bytes 1572868
  32.8 41.6 %collective-permute-start.3 = (bf16[256,4,128]{2,0,1:T(8,128)(2,1)}, bf16[256,4,128]{2,0,1:T(8,128)(2,1)S(1)}, u32[]{:S(2)}, u32[]{:S(2)}) collective-permute-start(bf16[256,4,128]{2,0,1:T(8,128)(2,1)} %multiply_convert_fusion.1), channel_id=1, source_target_pairs={{0,4},{4,8},{8,12},{12,16},{16,20},{20,24},{24,28},{1,5},{5,9},{9,... | collective-permute-start | bytes 786440 | tf_op jit(solution)/shard_map/ppermute | solution.py:19
  40.2 51.0 %collective-permute-start.5 = (bf16[256,4,128]{2,0,1:T(8,128)(2,1)S(1)}, bf16[256,4,128]{2,0,1:T(8,128)(2,1)}, u32[]{:S(2)}, u32[]{:S(2)}) collective-permute-start(bf16[256,4,128]{2,0,1:T(8,128)(2,1)S(1)} %copy.106), channel_id=1, source_target_pairs={{0,12},{4,16},{8,20},{12,24},{16,28},{1,13},{5,17},{9,21},{13,25},... | collective-permute-start | bytes 786440 | tf_op jit(solution)/shard_map/ppermute | solution.py:19
  58.6 31.4 %collective-permute-start.4 = (bf16[256,4,128]{2,0,1:T(8,128)(2,1)S(1)}, bf16[256,4,128]{2,0,1:T(8,128)(2,1)}, u32[]{:S(2)}, u32[]{:S(2)}) collective-permute-start(bf16[256,4,128]{2,0,1:T(8,128)(2,1)S(1)} %copy.106), channel_id=1, source_target_pairs={{0,16},{4,20},{8,24},{12,28},{1,17},{5,21},{9,25},{13,29},{2,18},{... | collective-permute-start | bytes 786440 | tf_op jit(solution)/shard_map/ppermute | solution.py:19
  156.6 7.7 %copy-start.9 = (f32[256,2,128]{2,0,1:T(8,128)S(1)}, f32[256,2,128]{2,0,1:T(8,128)}, u32[]{:S(2)}) copy-start(f32[256,2,128]{2,0,1:T(8,128)} %fusion.99) | copy-start | bytes 786436
  156.6 7.7 %copy-start.10 = (f32[256,2,128]{2,0,1:T(8,128)S(1)}, f32[256,2,128]{2,0,1:T(8,128)}, u32[]{:S(2)}) copy-start(f32[256,2,128]{2,0,1:T(8,128)} %fusion.102) | copy-start | bytes 786436
  156.6 7.7 %copy-start.11 = (f32[256,2,128]{2,0,1:T(8,128)S(1)}, f32[256,2,128]{2,0,1:T(8,128)}, u32[]{:S(2)}) copy-start(f32[256,2,128]{2,0,1:T(8,128)} %fusion.105) | copy-start | bytes 786436
  159.1 15.0 %collective-permute-start.12 = (bf16[256,4,128]{0,2,1:T(8,128)(2,1)}, bf16[256,4,128]{0,2,1:T(8,128)(2,1)}, u32[]{:S(2)}, u32[]{:S(2)}) collective-permute-start(bf16[256,4,128]{0,2,1:T(8,128)(2,1)} %get-tuple-element.27), channel_id=1, source_target_pairs={{4,0},{8,4},{12,8},{16,12},{20,16},{24,20},{28,24},{5,1},{9,5},{13... | collective-permute-start | bytes 786440 | tf_op jit(solution)/shard_map/ppermute | solution.py:19
  160.4 27.9 %collective-permute-start.15 = (bf16[256,4,128]{0,2,1:T(8,128)(2,1)}, bf16[256,4,128]{0,2,1:T(8,128)(2,1)}, u32[]{:S(2)}, u32[]{:S(2)}) collective-permute-start(bf16[256,4,128]{0,2,1:T(8,128)(2,1)} %get-tuple-element.28), channel_id=1, source_target_pairs={{16,0},{20,4},{24,8},{28,12},{17,1},{21,5},{25,9},{29,13},{18,2},{... | collective-permute-start | bytes 786440 | tf_op jit(solution)/shard_map/ppermute | solution.py:19
  161.7 27.9 %collective-permute-start.14 = (bf16[256,4,128]{0,2,1:T(8,128)(2,1)}, bf16[256,4,128]{0,2,1:T(8,128)(2,1)}, u32[]{:S(2)}, u32[]{:S(2)}) collective-permute-start(bf16[256,4,128]{0,2,1:T(8,128)(2,1)} %get-tuple-element.29), channel_id=1, source_target_pairs={{12,0},{16,4},{20,8},{24,12},{28,16},{13,1},{17,5},{21,9},{25,13},... | collective-permute-start | bytes 786440 | tf_op jit(solution)/shard_map/ppermute | solution.py:19
  163.0 27.9 %collective-permute-start.13 = (bf16[256,4,128]{0,2,1:T(8,128)(2,1)}, bf16[256,4,128]{0,2,1:T(8,128)(2,1)}, u32[]{:S(2)}, u32[]{:S(2)}) collective-permute-start(bf16[256,4,128]{0,2,1:T(8,128)(2,1)} %get-tuple-element.30), channel_id=1, source_target_pairs={{8,0},{12,4},{16,8},{20,12},{24,16},{28,20},{9,1},{13,5},{17,9},{2... | collective-permute-start | bytes 786440 | tf_op jit(solution)/shard_map/ppermute | solution.py:19
  172.8 20.3 %collective-permute-start.8 = (bf16[256,4,128]{2,0,1:T(8,128)(2,1)}, bf16[256,4,128]{2,0,1:T(8,128)(2,1)}, u32[]{:S(2)}, u32[]{:S(2)}) collective-permute-start(bf16[256,4,128]{2,0,1:T(8,128)(2,1)} %get-tuple-element.31), channel_id=1, source_target_pairs={{4,0},{8,4},{12,8},{16,12},{20,16},{24,20},{28,24},{5,1},{9,5},{13... | collective-permute-start | bytes 786440 | tf_op jit(solution)/shard_map/ppermute | solution.py:19
  174.1 42.2 %collective-permute-start.11 = (bf16[256,4,128]{2,0,1:T(8,128)(2,1)}, bf16[256,4,128]{2,0,1:T(8,128)(2,1)}, u32[]{:S(2)}, u32[]{:S(2)}) collective-permute-start(bf16[256,4,128]{2,0,1:T(8,128)(2,1)} %get-tuple-element.32), channel_id=1, source_target_pairs={{16,0},{20,4},{24,8},{28,12},{17,1},{21,5},{25,9},{29,13},{18,2},{... | collective-permute-start | bytes 786440 | tf_op jit(solution)/shard_map/ppermute | solution.py:19
  188.3 28.1 %collective-permute-start.10 = (bf16[256,4,128]{2,0,1:T(8,128)(2,1)}, bf16[256,4,128]{2,0,1:T(8,128)(2,1)}, u32[]{:S(2)}, u32[]{:S(2)}) collective-permute-start(bf16[256,4,128]{2,0,1:T(8,128)(2,1)} %get-tuple-element.33), channel_id=1, source_target_pairs={{12,0},{16,4},{20,8},{24,12},{28,16},{13,1},{17,5},{21,9},{25,13},... | collective-permute-start | bytes 786440 | tf_op jit(solution)/shard_map/ppermute | solution.py:19
  189.6 26.8 %collective-permute-start.9 = (bf16[256,4,128]{2,0,1:T(8,128)(2,1)}, bf16[256,4,128]{2,0,1:T(8,128)(2,1)}, u32[]{:S(2)}, u32[]{:S(2)}) collective-permute-start(bf16[256,4,128]{2,0,1:T(8,128)(2,1)} %get-tuple-element.34), channel_id=1, source_target_pairs={{8,0},{12,4},{16,8},{20,12},{24,16},{28,20},{9,1},{13,5},{17,9},{2... | collective-permute-start | bytes 786440 | tf_op jit(solution)/shard_map/ppermute | solution.py:19
  (6 other events, 22.6 us)
where the time goes:
time: 265 us; the launch traced here: 264 us
  matrix products  76.3 us (29%)
  starting transfers between devices  64.3 us (24%)
  waiting for transfers between devices  44.1 us (17%)
  blocking collectives  44.1 us (17%)
  local copies, waits for them, and re-layouts  20.6 us (8%)
  other arithmetic  13.5 us (5%)
    ppermute x16, starting transfers between devices, shifted(): return lax.ppermute(value, axis, pairs)  64.3 us
    ppermute x16, waiting for transfers between devices, shifted(): return lax.ppermute(value, axis, pairs)  44.1 us
    psum x1, blocking collectives, per_device(): gain_totals = lax.psum((q_gain_part, k_gain_part), ('ctx', 'tp'))  44.1 us
    dot_general x4, matrix products, per_device(): jnp.einsum('gtc,cd->tgd', dscores, head_keys, preferred_element_type=jnp....  23.4 us
    dot_general x4, matrix products, per_device(): jnp.einsum('gtc,tgd->cd', dscores, queries, preferred_element_type=jnp.fl...  22.4 us
    unnamed x43, local copies, waits for them, and re-layouts  16.3 us
    div x4, matrix products, per_device(): probs = exp_scores / jnp.sum(exp_scores, axis=-1, keepdims=True)  13.9 us
    dot_general x4, matrix products, per_device(): jnp.einsum('tgd,cd->gtc', grads, head_values, preferred_element_type=jnp....  11.4 us
  transfers between devices with their start and end apart: 16, of which 3 were waited for; matrix products, arithmetic and copies ran while one was open for 15% of the time, Pallas kernels for 0%

commit v1 on v0

v1 whole, which is shorter than its diff:
```python
import functools

import jax
import jax.numpy as jnp
from jax import lax
from jax.experimental import pallas as pl
from jax.experimental.pallas import tpu as pltpu
from jax.sharding import PartitionSpec as P

Q_HEADS = 32
KV_HEADS = 16
HEAD_DIM = 128
WINDOW = 1024

score_scale = 168.0 ** (-0.5)
epsilon = 1e-06
MESH = pl.DeviceIdType.MESH
F32 = jnp.float32
BF16 = jnp.bfloat16
T = 256
D = HEAD_DIM
BLOCKS = 5


def nt(a, b):
    return lax.dot_general(a, b, (((1,), (1,)), ((), ())), preferred_element_type=F32)


def tn(a, b):
    return lax.dot_general(a, b, (((0,), (0,)), ((), ())), preferred_element_type=F32)


def inverse_norm(x):
    return lax.rsqrt(jnp.mean(x * x, axis=-1, keepdims=True) + epsilon)


def norm_back(x, inv, gain, grad):
    unit = x * inv
    pulled = grad * gain
    raw = inv * (pulled - unit * jnp.mean(pulled * unit, axis=-1, keepdims=True))
    return raw, jnp.sum(grad * unit, axis=0, keepdims=True)


def kernel(n, m, q_in, k_in, v_in, g_in, qg, kg, dq_o, dk_o, dv_o, gain_o,
           q_b, g_b, k_b, v_b, kv, e_b, d_b, l_b, delta_b, dqt, acc, term, got, dq_s, dk_s, dv_s,
           gain_acc, gain_c, gain_t,
           x_loc, x_snd, x_rcv, f_snd, f_rcv, b_snd, b_rcv, o_loc, o_snd, o_rcv,
           p_loc, p_snd, p_rcv, c_snd, c_rcv, t_snd, t_rcv):
    c = lax.axis_index("ctx")
    tp = lax.axis_index("tp")
    x = lax.rem(c, 2)
    xp = c + 1 - 2 * x
    up = {"ctx": c + 2}
    down = {"ctx": c - 2}
    side = {"ctx": xp}
    has_next = c + 2 < n
    has_prev = c >= 2
    has_prev2 = c >= 4

    barrier = pltpu.get_barrier_semaphore()
    for k in range(1, n):
        pl.semaphore_signal(barrier, inc=1, device_id={"ctx": lax.rem(c + k, n)}, device_id_type=MESH)
    for k in range(1, m):
        pl.semaphore_signal(barrier, inc=1, device_id={"tp": lax.rem(tp + k, m)}, device_id_type=MESH)
    pl.semaphore_wait(barrier, n - 1 + m - 1)

    def remote(src, dst, snd, rcv, to):
        return pltpu.make_async_remote_copy(src_ref=src, dst_ref=dst, send_sem=snd, recv_sem=rcv,
                                            device_id=to, device_id_type=MESH)

    mine = pl.ds(pl.multiple_of(x * T, T), T)
    swaps = []
    for i, (src, dst, width) in enumerate(((k_in, k_b, 2 * D), (v_in, v_b, 2 * D), (q_in, q_b, 4 * D), (g_in, g_b, 4 * D))):
        there = pl.ds(pl.multiple_of((1 - x) * width, width), width)
        here = pl.ds(pl.multiple_of(x * width, width), width)
        far = remote(src.at[:, there], dst.at[mine, :], x_snd.at[i], x_rcv.at[i], side)
        near = pltpu.make_async_copy(src.at[:, here], dst.at[mine, :], x_loc.at[i])
        far.start()
        near.start()
        swaps.append((far, near))

    gain_acc[...] = jnp.zeros_like(gain_acc)
    acc[...] = jnp.zeros_like(acc)
    for far, near in swaps[:2]:
        near.wait()
        far.wait_recv()
    own = pl.ds(4 * T, 2 * T)
    one = pl.ds(2 * T, 2 * T)
    two = pl.ds(0, 2 * T)

    def send_own(h):
        return remote(kv.at[h, :, own], kv.at[h, :, one], f_snd.at[h, 0], f_rcv.at[h, 0], up)

    def send_on(h):
        return remote(kv.at[h, :, one], kv.at[h, :, two], f_snd.at[h, 1], f_rcv.at[h, 1], up)

    def back_two(h):
        return remote(term.at[h, 0], got.at[h, 0], b_snd.at[h, 0], b_rcv.at[h, 0], down)

    def back_one(h):
        return remote(term.at[h, 1], got.at[h, 1], b_snd.at[h, 1], b_rcv.at[h, 1], down)

    def forward(h):
        @pl.when(has_prev)
        def _():
            send_own(h).wait_recv()

        @pl.when(has_prev & has_next)
        def _():
            send_on(h).start()

    for h in range(2):
        cols = slice(h * D, (h + 1) * D)
        raw = k_b[:, cols].astype(F32)
        kv[h, 0, 4 * T : 6 * T, :] = (raw * inverse_norm(raw) * kg[...]).astype(BF16)
        kv[h, 1, 4 * T : 6 * T, :] = v_b[:, cols]
        if h == 0:
            @pl.when(has_next)
            def _():
                send_own(0).start()

    forward(0)

    @pl.when(has_next)
    def _():
        send_own(1).start()

    for far, near in swaps[2:]:
        near.wait()
        far.wait_recv()

    row = lax.broadcasted_iota(jnp.int32, (T, 2 * T), 0)
    col = lax.rem(lax.broadcasted_iota(jnp.int32, (T, 2 * T), 1), T)

    def attend(s):
        h = s // 2
        qb = lax.rem(s, 2)
        rows = pl.ds(pl.multiple_of(qb * T, T), T)
        col0 = pl.ds(pl.multiple_of(h * 2 * D, D), D)
        col1 = pl.ds(pl.multiple_of(h * 2 * D + D, D), D)
        raw = jnp.concatenate([q_b[rows, col0], q_b[rows, col1]], axis=0).astype(F32)
        grads = jnp.concatenate([g_b[rows, col0], g_b[rows, col1]], axis=0)
        inv = inverse_norm(raw)
        queries = (raw * inv * qg[...]).astype(BF16)
        l_b[...] = jnp.zeros_like(l_b)
        delta_b[...] = jnp.zeros_like(delta_b)
        dqt[...] = jnp.zeros_like(dqt)

        def keyed(i, body):
            start = pl.multiple_of((qb + i) * T, T)
            if i == BLOCKS - 1:
                body(i, pl.ds(start, T))
            else:
                @pl.when(c - x - 4 + qb + i >= 0)
                def _():
                    body(i, pl.ds(start, T))

        def first(i, keys):
            scores = nt(kv[h, 0, keys, :], queries)
            e = jnp.exp(scores * score_scale)
            if i == 0:
                e = jnp.where(col < row, e, 0.0)
            if i == BLOCKS - 1:
                e = jnp.where(col >= row, e, 0.0)
            dp = nt(kv[h, 1, keys, :], grads)
            e_b[i] = e
            d_b[i] = dp
            l_b[...] += jnp.sum(e, axis=0, keepdims=True)
            delta_b[...] += jnp.sum(e * dp, axis=0, keepdims=True)

        for i in reversed(range(BLOCKS)):
            keyed(i, first)
        il = 1.0 / l_b[...]
        delta = delta_b[...] * il

        def second(i, keys):
            p = e_b[i] * il
            ds = (p * (d_b[i] - delta) * score_scale).astype(BF16)
            acc[h, 0, keys, :] += jnp.dot(ds, queries, preferred_element_type=F32)
            acc[h, 1, keys, :] += jnp.dot(p.astype(BF16), grads, preferred_element_type=F32)
            dqt[...] += tn(kv[h, 0, keys, :], ds)

        for i in range(BLOCKS):
            keyed(i, second)
        dq = jnp.transpose(dqt[...])
        dq_raw, gain_part = norm_back(raw, inv, qg[...], dq)
        gain_acc[0:1, :] += gain_part
        dq_raw = dq_raw.astype(BF16)
        dq_s[s, :, 0:D] = dq_raw[0:T]
        dq_s[s, :, D : 2 * D] = dq_raw[T : 2 * T]

        @pl.when(qb == x)
        def _():
            put_local(h, s).start()

        @pl.when(qb != x)
        def _():
            put_remote(h, s).start()

    def dq_place(h):
        return dq_o.at[:, pl.ds(pl.multiple_of(x * 4 * D + h * 2 * D, 2 * D), 2 * D)]

    def put_local(h, s):
        return pltpu.make_async_copy(dq_s.at[s], dq_place(h), o_loc.at[h])

    def put_remote(h, s):
        return remote(dq_s.at[s], dq_place(h), o_snd.at[h], o_rcv.at[h], side)

    def start_two(h):
        @pl.when(has_prev2)
        def _():
            term[h, 0] = acc[h, :, 0 : 2 * T, :].astype(BF16)
            back_two(h).start()

    def start_one(h):
        @pl.when(has_prev & has_next)
        def _():
            back_two(h).wait_recv()
            term[h, 1] = (acc[h, :, 2 * T : 4 * T, :] + got[h, 0].astype(F32)).astype(BF16)

        @pl.when(has_prev & jnp.logical_not(has_next))
        def _():
            term[h, 1] = acc[h, :, 2 * T : 4 * T, :].astype(BF16)

        @pl.when(has_prev)
        def _():
            back_one(h).start()

    def outs(h):
        place = pl.ds(pl.multiple_of(x * 2 * D + h * D, D), D)
        other = pl.ds(pl.multiple_of((1 - x) * T, T), T)
        made = []
        for i, (src, dst) in enumerate(((dk_s, dk_o), (dv_s, dv_o))):
            made.append(pltpu.make_async_copy(src.at[h, mine], dst.at[:, place], p_loc.at[h, i]))
            made.append(remote(src.at[h, other], dst.at[:, place], p_snd.at[h, i], p_rcv.at[h, i], side))
        return made

    def finish(h):
        @pl.when(has_next)
        def _():
            back_one(h).wait_recv()
            acc[h, :, 4 * T : 6 * T, :] += got[h, 1].astype(F32)

        raw = k_b[:, h * D : (h + 1) * D].astype(F32)
        dk_raw, gain_part = norm_back(raw, inverse_norm(raw), kg[...], acc[h, 0, 4 * T : 6 * T, :])
        gain_acc[1:2, :] += gain_part
        dk_s[h] = dk_raw.astype(BF16)
        dv_s[h] = acc[h, 1, 4 * T : 6 * T, :].astype(BF16)
        for copy in outs(h):
            copy.start()

    def step(s, carry):
        @pl.when((s == 0) & has_prev2)
        def _():
            send_on(0).wait_recv()

        @pl.when(s == 1)
        def _():
            forward(1)

        @pl.when((s == 2) & has_prev2)
        def _():
            send_on(1).wait_recv()

        attend(s)

        @pl.when(s == 1)
        def _():
            start_two(0)

        @pl.when(s == 2)
        def _():
            start_one(0)

        return carry

    lax.fori_loop(0, 4, step, 0)
    start_two(1)
    finish(0)
    start_one(1)
    finish(1)

    def spread(size, me, axis, buf, snd, rcv):
        copies = []
        for k in range(1, size):
            copies.append(remote(buf.at[me], buf.at[me], snd.at[k], rcv.at[k], {axis: lax.rem(me + k, size)}))
        for copy in copies:
            copy.start()
        for copy in copies:
            copy.wait_recv()
        return copies

    gain_c[c] = gain_acc[...]
    sent = spread(n, c, "ctx", gain_c, c_snd, c_rcv)
    gain_t[tp] = jnp.sum(gain_c[...], axis=0)
    sent += spread(m, tp, "tp", gain_t, t_snd, t_rcv)
    total = jnp.sum(gain_t[...], axis=0)
    gain_o[0:1, :] = total[0:1] * ((n * T * Q_HEADS) ** -0.5)
    gain_o[1:2, :] = total[1:2] * ((n * T * KV_HEADS) ** -0.5)

    for copy in sent:
        copy.wait_send()
    for far, _ in swaps:
        far.wait_send()
    for h in range(2):
        @pl.when(has_next)
        def _():
            send_own(h).wait_send()

        @pl.when(has_prev & has_next)
        def _():
            send_on(h).wait_send()

        @pl.when(has_prev2)
        def _():
            back_two(h).wait_send()

        @pl.when(has_prev)
        def _():
            back_one(h).wait_send()

        put_local(h, 2 * h + x).wait()
        put_remote(h, 2 * h + 1 - x).wait()
        for copy in outs(h):
            copy.wait()


def per_device(n, m, q_raw, k_raw, v_cur, d_out, q_gain, k_gain):
    dma = pltpu.SemaphoreType.DMA
    anywhere = pl.BlockSpec(memory_space=pl.ANY)
    vmem = pl.BlockSpec(memory_space=pltpu.VMEM)
    dq_raw, dk_raw, dv, gains = pl.pallas_call(
        functools.partial(kernel, n, m),
        out_shape=(
            jax.ShapeDtypeStruct(q_raw.shape, BF16),
            jax.ShapeDtypeStruct(k_raw.shape, BF16),
            jax.ShapeDtypeStruct(v_cur.shape, BF16),
            jax.ShapeDtypeStruct((2, D), F32),
        ),
        in_specs=[anywhere] * 4 + [vmem] * 2,
        out_specs=(anywhere, anywhere, anywhere, vmem),
        scratch_shapes=[
            pltpu.VMEM((2 * T, 4 * D), BF16),
            pltpu.VMEM((2 * T, 4 * D), BF16),
            pltpu.VMEM((2 * T, 2 * D), BF16),
            pltpu.VMEM((2 * T, 2 * D), BF16),
            pltpu.VMEM((2, 2, 6 * T, D), BF16),
            pltpu.VMEM((BLOCKS, T, 2 * T), F32),
            pltpu.VMEM((BLOCKS, T, 2 * T), F32),
            pltpu.VMEM((1, 2 * T), F32),
            pltpu.VMEM((1, 2 * T), F32),
            pltpu.VMEM((D, 2 * T), F32),
            pltpu.VMEM((2, 2, 6 * T, D), F32),
            pltpu.VMEM((2, 2, 2, 2 * T, D), BF16),
            pltpu.VMEM((2, 2, 2, 2 * T, D), BF16),
            pltpu.VMEM((4, T, 2 * D), BF16),
            pltpu.VMEM((2, 2 * T, D), BF16),
            pltpu.VMEM((2, 2 * T, D), BF16),
            pltpu.VMEM((8, D), F32),
            pltpu.VMEM((n, 8, D), F32),
            pltpu.VMEM((m, 8, D), F32),
            dma((4,)), dma((4,)), dma((4,)),
            dma((2, 2)), dma((2, 2)), dma((2, 2)), dma((2, 2)),
            dma((2,)), dma((2,)), dma((2,)),
            dma((2, 2)), dma((2, 2)), dma((2, 2)),
            dma((n,)), dma((n,)), dma((m,)), dma((m,)),
        ],
        compiler_params=pltpu.CompilerParams(
            collective_id=0, has_side_effects=True, vmem_limit_bytes=48 * 1024 * 1024
        ),
    )(q_raw, k_raw, v_cur, d_out, q_gain.reshape(1, D), k_gain.reshape(1, D))
    return (dq_raw, dk_raw, dv, gains[0], gains[1])


def solution(mesh):
    return jax.shard_map(
        functools.partial(per_device, mesh.shape["ctx"], mesh.shape["tp"]),
        mesh=mesh,
        in_specs=(P("ctx", "tp"), P("ctx", "tp"), P("ctx", "tp"), P("ctx", "tp"), P(), P()),
        out_specs=(P("ctx", "tp"), P("ctx", "tp"), P("ctx", "tp"), P(), P()),
        check_vma=False,
    )
```

time: 265 us -> 77.9 us (0.29)
  matrix products: 76.3 us -> 0 us
  Pallas kernels: 0 us -> 69.6 us
  starting transfers between devices: 64.3 us -> 0 us
  blocking collectives: 44.1 us -> 0 us
  waiting for transfers between devices: 44.1 us -> 0 us
  other arithmetic: 13.5 us -> 0 us
  local copies, waits for them, and re-layouts: 20.6 us -> 7.35 us
    pallas_call x0 -> x1, Pallas kernels: none -> 69.6 us  [per_device(): pl.pallas_call(functools.partial(kernel, n, m), out_shape=(jax.ShapeDtype...]
    ppermute x16 -> x0, starting transfers between devices: 64.3 us -> none  [shifted(): return lax.ppermute(value, axis, pairs)]
    dot_general x16 -> x0, matrix products: 62.4 us -> none  [the longest x4 23.4 us: per_device(): jnp.einsum('gtc,cd->tgd', dscores, head_keys, preferred_element_type=jnp....]
    ppermute x16 -> x0, waiting for transfers between devices: 44.1 us -> none  [shifted(): return lax.ppermute(value, axis, pairs)]
    psum x1 -> x0, blocking collectives: 44.1 us -> none  [per_device(): gain_totals = lax.psum((q_gain_part, k_gain_part), ('ctx', 'tp'))]
    div x4 -> x0, matrix products: 13.9 us -> none  [per_device(): probs = exp_scores / jnp.sum(exp_scores, axis=-1, keepdims=True)]
    unnamed x43 -> x15, local copies, waits for them, and re-layouts: 16.3 us -> 6.83 us
    reduce_sum x6 -> x0, other arithmetic: 4.22 us -> none  [the longest x4 4.04 us: normalize(): return vectors * inverse * gain]
  transfers between devices with their start and end apart: 16 -> 0, of which waited for: 3 -> 0; matrix products, arithmetic and copies ran while one was open for 15% -> 0% of each run, Pallas kernels for 0% -> 0%
where the time goes in v1:
time: 77.9 us; the launch traced here: 77.6 us
  Pallas kernels  69.6 us (89%)
  local copies, waits for them, and re-layouts  7.35 us (9%)
    pallas_call x1, Pallas kernels, per_device(): pl.pallas_call(functools.partial(kernel, n, m), out_shape=(jax.ShapeDtype...  69.6 us
    unnamed x15, local copies, waits for them, and re-layouts  6.83 us

profile of v1, /device:TPU:0, one launch (start us, length us, event | category | flops | bytes accessed | tf_op | source)
XLA Modules:
  0.0 77.6 jit_solution(16348183993885898741)
XLA Ops:
  0.6 0.0 copy-start.4
  0.6 0.0 copy-start.5
  0.7 0.6 copy-done.4
  1.3 0.0 copy-done.5
  1.3 0.0 copy-start
  1.3 1.0 %copy-done = bf16[256,1024]{1,0:T(8,128)(2,1)S(1)} copy-done((bf16[256,1024]{1,0:T(8,128)(2,1)S(1)}, bf16[256,1024]{1,0:T(8,128)(2,1)}, u32[]{:S(2)}) %copy-start) | copy-done | bytes 524312
  2.3 0.0 copy-start.1
  2.3 1.0 %copy-done.1 = bf16[256,1024]{1,0:T(8,128)(2,1)S(1)} copy-done((bf16[256,1024]{1,0:T(8,128)(2,1)S(1)}, bf16[256,1024]{1,0:T(8,128)(2,1)}, u32[]{:S(2)}) %copy-start.1) | copy-done | bytes 524312
  3.4 0.0 copy-start.2
  3.4 0.9 %copy-done.2 = bf16[256,512]{1,0:T(8,128)(2,1)S(1)} copy-done((bf16[256,512]{1,0:T(8,128)(2,1)S(1)}, bf16[256,512]{1,0:T(8,128)(2,1)}, u32[]{:S(2)}) %copy-start.2) | copy-done | bytes 262168
  4.3 0.0 copy-start.3
  4.3 0.9 %copy-done.3 = bf16[256,512]{1,0:T(8,128)(2,1)S(1)} copy-done((bf16[256,512]{1,0:T(8,128)(2,1)S(1)}, bf16[256,512]{1,0:T(8,128)(2,1)}, u32[]{:S(2)}) %copy-start.3) | copy-done | bytes 262168
  5.3 69.6 %shard_map.101 = (bf16[256,1024]{1,0:T(8,128)(2,1)S(1)}, bf16[256,512]{1,0:T(8,128)(2,1)S(1)}, bf16[256,512]{1,0:T(8,128)(2,1)S(1)}, f32[2,128]{1,0:T(2,128)S(1)}) custom-call(bf16[256,1024]{1,0:T(8,128)(2,1)S(1)} %copy-done, bf16[256,512]{1,0:T(8,128)(2,1)S(1)} %copy-done.2, bf16[256,512]{1,0:T(8,128)(2,1)S(1)} %copy-done.3, ...), custom_call_target="tpu_custom_call" | custom-call | tf_op jit(solution)/shard_map/pallas_call | solution.py:332
  74.9 0.5 slice_bitcast_fusion
  75.4 0.8 %copy.14 = bf16[256,1024]{1,0:T(8,128)(2,1)} copy(bf16[256,1024]{1,0:T(8,128)(2,1)S(1)} %get-tuple-element.20) | data formatting | bytes 1048576
  76.2 0.7 copy.15
  76.9 0.7 copy.16
Async XLA Ops:
  0.6 0.7 copy-start.4
  0.6 0.7 copy-start.5
  1.3 1.0 %copy-start = (bf16[256,1024]{1,0:T(8,128)(2,1)S(1)}, bf16[256,1024]{1,0:T(8,128)(2,1)}, u32[]{:S(2)}) copy-start(bf16[256,1024]{1,0:T(8,128)(2,1)} %q_in.1) | copy-start | bytes 1572868
  2.3 1.0 %copy-start.1 = (bf16[256,1024]{1,0:T(8,128)(2,1)S(1)}, bf16[256,1024]{1,0:T(8,128)(2,1)}, u32[]{:S(2)}) copy-start(bf16[256,1024]{1,0:T(8,128)(2,1)} %g_in.1) | copy-start | bytes 1572868
  3.4 0.9 %copy-start.2 = (bf16[256,512]{1,0:T(8,128)(2,1)S(1)}, bf16[256,512]{1,0:T(8,128)(2,1)}, u32[]{:S(2)}) copy-start(bf16[256,512]{1,0:T(8,128)(2,1)} %k_in.1) | copy-start | bytes 786436
  4.3 0.9 %copy-start.3 = (bf16[256,512]{1,0:T(8,128)(2,1)S(1)}, bf16[256,512]{1,0:T(8,128)(2,1)}, u32[]{:S(2)}) copy-start(bf16[256,512]{1,0:T(8,128)(2,1)} %v_in.1) | copy-start | bytes 786436

commit v2 on v1

--- a/solution.py
+++ b/solution.py
@@ -69,65 +69,83 @@
                                             device_id=to, device_id_type=MESH)
 
     mine = pl.ds(pl.multiple_of(x * T, T), T)
-    swaps = []
-    for i, (src, dst, width) in enumerate(((k_in, k_b, 2 * D), (v_in, v_b, 2 * D), (q_in, q_b, 4 * D), (g_in, g_b, 4 * D))):
-        there = pl.ds(pl.multiple_of((1 - x) * width, width), width)
-        here = pl.ds(pl.multiple_of(x * width, width), width)
-        far = remote(src.at[:, there], dst.at[mine, :], x_snd.at[i], x_rcv.at[i], side)
-        near = pltpu.make_async_copy(src.at[:, here], dst.at[mine, :], x_loc.at[i])
-        far.start()
-        near.start()
-        swaps.append((far, near))
-
+    theirs = pl.ds(pl.multiple_of((1 - x) * T, T), T)
+
+    def swap(i, src, dst, h, width):
+        there = pl.ds(pl.multiple_of((1 - x) * 2 * width + h * width, D), width)
+        here = pl.ds(pl.multiple_of(x * 2 * width + h * width, D), width)
+        cols = slice(h * width, (h + 1) * width)
+        return (remote(src.at[:, there], dst.at[mine, cols], x_snd.at[i, h], x_rcv.at[i, h], side),
+                pltpu.make_async_copy(src.at[:, here], dst.at[mine, cols], x_loc.at[i, h]))
+
+    keys_in = [[swap(0, k_in, k_b, h, D), swap(1, v_in, v_b, h, D)] for h in range(2)]
+    rows_in = [[swap(2, q_in, q_b, h, 2 * D), swap(3, g_in, g_b, h, 2 * D)] for h in range(2)]
+    for h in range(2):
+        for far, near in keys_in[h]:
+            near.start()
+            far.start()
+
+    def half_rows(hop, half):
+        return pl.ds(pl.multiple_of((4 - 2 * hop) * T + half * T, T), T)
+
+    def send_own(h, half):
+        return remote(kv.at[h, :, half_rows(0, half)], kv.at[h, :, half_rows(1, half)],
+                      f_snd.at[h, 0, half], f_rcv.at[h, 0, half], up)
+
+    def send_on(h, half):
+        return remote(kv.at[h, :, half_rows(1, half)], kv.at[h, :, half_rows(2, half)],
+                      f_snd.at[h, 1, half], f_rcv.at[h, 1, half], up)
+
+    def back_two(h, half):
+        return remote(term.at[h, 0, half], got.at[h, 0, half], b_snd.at[h, 0, half], b_rcv.at[h, 0, half], down)
+
+    def back_one(h, half):
+        return remote(term.at[h, 1, half], got.at[h, 1, half], b_snd.at[h, 1, half], b_rcv.at[h, 1, half], down)
+
+    def forward(h, half):
+        @pl.when(has_prev)
+        def _():
+            send_own(h, half).wait_recv()
+
+        @pl.when(has_prev & has_next)
+        def _():
+            send_on(h, half).start()
+
+    def fill(h, half, rows):
+        cols = slice(h * D, (h + 1) * D)
+        raw = k_b[rows, cols].astype(F32)
+        kv[h, 0, half_rows(0, half), :] = (raw * inverse_norm(raw) * kg[...]).astype(BF16)
+        kv[h, 1, half_rows(0, half), :] = v_b[rows, cols]
+
+    def start_own(h, half):
+        @pl.when(has_next)
+        def _():
+            send_own(h, half).start()
+
+    for far, near in keys_in[0]:
+        near.wait()
+    fill(0, x, mine)
+    start_own(0, x)
+    for far, near in keys_in[1]:
+        near.wait()
+    fill(1, x, mine)
     gain_acc[...] = jnp.zeros_like(gain_acc)
+    for far, near in keys_in[0]:
+        far.wait_recv()
+    fill(0, 1 - x, theirs)
+    start_own(0, 1 - x)
+    for far, near in keys_in[1]:
+        far.wait_recv()
+    for h in range(2):
+        for far, near in rows_in[h]:
+            near.start()
+            far.start()
+    fill(1, 1 - x, theirs)
+    forward(0, x)
+    forward(0, 1 - x)
+    start_own(1, x)
+    start_own(1, 1 - x)
     acc[...] = jnp.zeros_like(acc)
-    for far, near in swaps[:2]:
-        near.wait()
-        far.wait_recv()
-    own = pl.ds(4 * T, 2 * T)
-    one = pl.ds(2 * T, 2 * T)
-    two = pl.ds(0, 2 * T)
-
-    def send_own(h):
-        return remote(kv.at[h, :, own], kv.at[h, :, one], f_snd.at[h, 0], f_rcv.at[h, 0], up)
-
-    def send_on(h):
-        return remote(kv.at[h, :, one], kv.at[h, :, two], f_snd.at[h, 1], f_rcv.at[h, 1], up)
-
-    def back_two(h):
-        return remote(term.at[h, 0], got.at[h, 0], b_snd.at[h, 0], b_rcv.at[h, 0], down)
-
-    def back_one(h):
-        return remote(term.at[h, 1], got.at[h, 1], b_snd.at[h, 1], b_rcv.at[h, 1], down)
-
-    def forward(h):
-        @pl.when(has_prev)
-        def _():
-            send_own(h).wait_recv()
-
-        @pl.when(has_prev & has_next)
-        def _():
-            send_on(h).start()
-
-    for h in range(2):
-        cols = slice(h * D, (h + 1) * D)
-        raw = k_b[:, cols].astype(F32)
-        kv[h, 0, 4 * T : 6 * T, :] = (raw * inverse_norm(raw) * kg[...]).astype(BF16)
-        kv[h, 1, 4 * T : 6 * T, :] = v_b[:, cols]
-        if h == 0:
-            @pl.when(has_next)
-            def _():
-                send_own(0).start()
-
-    forward(0)
-
-    @pl.when(has_next)
-    def _():
-        send_own(1).start()
-
-    for far, near in swaps[2:]:
-        near.wait()
-        far.wait_recv()
 
     row = lax.broadcasted_iota(jnp.int32, (T, 2 * T), 0)
     col = lax.rem(lax.broadcasted_iota(jnp.int32, (T, 2 * T), 1), T)
@@ -206,79 +224,112 @@
     def put_remote(h, s):
         return remote(dq_s.at[s], dq_place(h), o_snd.at[h], o_rcv.at[h], side)
 
-    def start_two(h):
+    def start_two(h, half):
         @pl.when(has_prev2)
         def _():
-            term[h, 0] = acc[h, :, 0 : 2 * T, :].astype(BF16)
-            back_two(h).start()
-
-    def start_one(h):
+            term[h, 0, half] = acc[h, :, half_rows(2, half), :].astype(BF16)
+            back_two(h, half).start()
+
+    def start_one(h, half):
         @pl.when(has_prev & has_next)
         def _():
-            back_two(h).wait_recv()
-            term[h, 1] = (acc[h, :, 2 * T : 4 * T, :] + got[h, 0].astype(F32)).astype(BF16)
+            back_two(h, half).wait_recv()
+            term[h, 1, half] = (acc[h, :, half_rows(1, half), :] + got[h, 0, half].astype(F32)).astype(BF16)
 
         @pl.when(has_prev & jnp.logical_not(has_next))
         def _():
-            term[h, 1] = acc[h, :, 2 * T : 4 * T, :].astype(BF16)
+            term[h, 1, half] = acc[h, :, half_rows(1, half), :].astype(BF16)
 
         @pl.when(has_prev)
         def _():
-            back_one(h).start()
-
-    def outs(h):
-        place = pl.ds(pl.multiple_of(x * 2 * D + h * D, D), D)
-        other = pl.ds(pl.multiple_of((1 - x) * T, T), T)
-        made = []
-        for i, (src, dst) in enumerate(((dk_s, dk_o), (dv_s, dv_o))):
-            made.append(pltpu.make_async_copy(src.at[h, mine], dst.at[:, place], p_loc.at[h, i]))
-            made.append(remote(src.at[h, other], dst.at[:, place], p_snd.at[h, i], p_rcv.at[h, i], side))
-        return made
-
-    def finish(h):
+            back_one(h, half).start()
+
+    def place(dst, h):
+        return dst.at[:, pl.ds(pl.multiple_of(x * 2 * D + h * D, D), D)]
+
+    def keep(h):
+        return [pltpu.make_async_copy(src.at[h, mine], place(dst, h), p_loc.at[h, i])
+                for i, (src, dst) in enumerate(((dk_s, dk_o), (dv_s, dv_o)))]
+
+    def give(h):
+        return [remote(src.at[h, theirs], place(dst, h), p_snd.at[h, i], p_rcv.at[h, i], side)
+                for i, (src, dst) in enumerate(((dk_s, dk_o), (dv_s, dv_o)))]
+
+    def finish(h, half):
+        rows = pl.ds(pl.multiple_of(half * T, T), T)
+        here = half_rows(0, half)
+
         @pl.when(has_next)
         def _():
-            back_one(h).wait_recv()
-            acc[h, :, 4 * T : 6 * T, :] += got[h, 1].astype(F32)
-
-        raw = k_b[:, h * D : (h + 1) * D].astype(F32)
-        dk_raw, gain_part = norm_back(raw, inverse_norm(raw), kg[...], acc[h, 0, 4 * T : 6 * T, :])
+            back_one(h, half).wait_recv()
+            acc[h, :, here, :] += got[h, 1, half].astype(F32)
+
+        raw = k_b[rows, h * D : (h + 1) * D].astype(F32)
+        dk_raw, gain_part = norm_back(raw, inverse_norm(raw), kg[...], acc[h, 0, here, :])
         gain_acc[1:2, :] += gain_part
-        dk_s[h] = dk_raw.astype(BF16)
-        dv_s[h] = acc[h, 1, 4 * T : 6 * T, :].astype(BF16)
-        for copy in outs(h):
-            copy.start()
+        dk_s[h, rows] = dk_raw.astype(BF16)
+        dv_s[h, rows] = acc[h, 1, here, :].astype(BF16)
+
+        @pl.when(x == half)
+        def _():
+            for copy in keep(h):
+                copy.start()
+
+        @pl.when(x != half)
+        def _():
+            for copy in give(h):
+                copy.start()
+
+    def arrived(h):
+        @pl.when(has_prev2)
+        def _():
+            send_on(h, 0).wait_recv()
+            send_on(h, 1).wait_recv()
+
+        for far, near in rows_in[h]:
+            near.wait()
+            far.wait_recv()
 
     def step(s, carry):
-        @pl.when((s == 0) & has_prev2)
-        def _():
-            send_on(0).wait_recv()
+        @pl.when(s == 0)
+        def _():
+            arrived(0)
 
         @pl.when(s == 1)
         def _():
-            forward(1)
-
-        @pl.when((s == 2) & has_prev2)
-        def _():
-            send_on(1).wait_recv()
+            forward(1, x)
+            forward(1, 1 - x)
+
+        @pl.when(s == 2)
+        def _():
+            arrived(1)
 
         attend(s)
 
+        @pl.when(s == 0)
+        def _():
+            start_two(0, 0)
+
         @pl.when(s == 1)
         def _():
-            start_two(0)
+            start_two(0, 1)
+            start_one(0, 0)
 
         @pl.when(s == 2)
         def _():
-            start_one(0)
+            start_one(0, 1)
+            start_two(1, 0)
 
         return carry
 
     lax.fori_loop(0, 4, step, 0)
-    start_two(1)
-    finish(0)
-    start_one(1)
-    finish(1)
+    start_two(1, 1)
+    start_one(1, 0)
+    finish(0, 0)
+    finish(0, 1)
+    start_one(1, 1)
+    finish(1, 0)
+    finish(1, 1)
 
     def spread(size, me, axis, buf, snd, rcv):
         copies = []
@@ -300,28 +351,29 @@
 
     for copy in sent:
         copy.wait_send()
-    for far, _ in swaps:
-        far.wait_send()
     for h in range(2):
-        @pl.when(has_next)
-        def _():
-            send_own(h).wait_send()
-
-        @pl.when(has_prev & has_next)
-        def _():
-            send_on(h).wait_send()
-
-        @pl.when(has_prev2)
-        def _():
-            back_two(h).wait_send()
-
-        @pl.when(has_prev)
-        def _():
-            back_one(h).wait_send()
+        for far, _ in keys_in[h] + rows_in[h]:
+            far.wait_send()
+        for half in range(2):
+            @pl.when(has_next)
+            def _():
+                send_own(h, half).wait_send()
+
+            @pl.when(has_prev & has_next)
+            def _():
+                send_on(h, half).wait_send()
+
+            @pl.when(has_prev2)
+            def _():
+                back_two(h, half).wait_send()
+
+            @pl.when(has_prev)
+            def _():
+                back_one(h, half).wait_send()
 
         put_local(h, 2 * h + x).wait()
         put_remote(h, 2 * h + 1 - x).wait()
-        for copy in outs(h):
+        for copy in keep(h) + give(h):
             copy.wait()
 
 
@@ -337,7 +389,7 @@
             jax.ShapeDtypeStruct(v_cur.shape, BF16),
             jax.ShapeDtypeStruct((2, D), F32),
         ),
-        in_specs=[anywhere] * 4 + [vmem] * 2,
+        in_specs=[pl.BlockSpec(memory_space=pltpu.HBM)] * 4 + [vmem] * 2,
         out_specs=(anywhere, anywhere, anywhere, vmem),
         scratch_shapes=[
             pltpu.VMEM((2 * T, 4 * D), BF16),
@@ -351,16 +403,16 @@
             pltpu.VMEM((1, 2 * T), F32),
             pltpu.VMEM((D, 2 * T), F32),
             pltpu.VMEM((2, 2, 6 * T, D), F32),
-            pltpu.VMEM((2, 2, 2, 2 * T, D), BF16),
-            pltpu.VMEM((2, 2, 2, 2 * T, D), BF16),
+            pltpu.VMEM((2, 2, 2, 2, T, D), BF16),
+            pltpu.VMEM((2, 2, 2, 2, T, D), BF16),
             pltpu.VMEM((4, T, 2 * D), BF16),
             pltpu.VMEM((2, 2 * T, D), BF16),
             pltpu.VMEM((2, 2 * T, D), BF16),
             pltpu.VMEM((8, D), F32),
             pltpu.VMEM((n, 8, D), F32),
             pltpu.VMEM((m, 8, D), F32),
-            dma((4,)), dma((4,)), dma((4,)),
-            dma((2, 2)), dma((2, 2)), dma((2, 2)), dma((2, 2)),
+            dma((4, 2)), dma((4, 2)), dma((4, 2)),
+            dma((2, 2, 2)), dma((2, 2, 2)), dma((2, 2, 2)), dma((2, 2, 2)),
             dma((2,)), dma((2,)), dma((2,)),
             dma((2, 2)), dma((2, 2)), dma((2, 2)),
             dma((n,)), dma((n,)), dma((m,)), dma((m,)),

time: 77.9 us -> 67 us (0.86)
  Pallas kernels: 69.6 us -> 58.7 us
    pallas_call x1, Pallas kernels: 69.6 us -> 58.7 us  [per_device(): pl.pallas_call(functools.partial(kernel, n, m), out_shape=(jax.ShapeDtype...]
where the time goes in v2:
time: 67 us; the launch traced here: 66.8 us
  Pallas kernels  58.7 us (88%)
  local copies, waits for them, and re-layouts  7.35 us (11%)
    pallas_call x1, Pallas kernels, per_device(): pl.pallas_call(functools.partial(kernel, n, m), out_shape=(jax.ShapeDtype...  58.7 us
    unnamed x15, local copies, waits for them, and re-layouts  6.83 us

profile of v2, /device:TPU:0, one launch (start us, length us, event | category | flops | bytes accessed | tf_op | source)
XLA Modules:
  0.0 66.8 jit_solution(1694851333301737900)
XLA Ops:
  0.6 0.0 copy-start.4
  0.6 0.0 copy-start.5
  0.7 0.6 copy-done.4
  1.3 0.0 copy-done.5
  1.3 0.0 copy-start
  1.3 1.0 %copy-done = bf16[256,1024]{1,0:T(8,128)(2,1)S(1)} copy-done((bf16[256,1024]{1,0:T(8,128)(2,1)S(1)}, bf16[256,1024]{1,0:T(8,128)(2,1)}, u32[]{:S(2)}) %copy-start) | copy-done | bytes 524312
  2.3 0.0 copy-start.1
  2.3 1.0 %copy-done.1 = bf16[256,1024]{1,0:T(8,128)(2,1)S(1)} copy-done((bf16[256,1024]{1,0:T(8,128)(2,1)S(1)}, bf16[256,1024]{1,0:T(8,128)(2,1)}, u32[]{:S(2)}) %copy-start.1) | copy-done | bytes 524312
  3.4 0.0 copy-start.2
  3.4 0.9 %copy-done.2 = bf16[256,512]{1,0:T(8,128)(2,1)S(1)} copy-done((bf16[256,512]{1,0:T(8,128)(2,1)S(1)}, bf16[256,512]{1,0:T(8,128)(2,1)}, u32[]{:S(2)}) %copy-start.2) | copy-done | bytes 262168
  4.3 0.0 copy-start.3
  4.3 0.9 %copy-done.3 = bf16[256,512]{1,0:T(8,128)(2,1)S(1)} copy-done((bf16[256,512]{1,0:T(8,128)(2,1)S(1)}, bf16[256,512]{1,0:T(8,128)(2,1)}, u32[]{:S(2)}) %copy-start.3) | copy-done | bytes 262168
  5.3 58.7 %shard_map.101 = (bf16[256,1024]{1,0:T(8,128)(2,1)S(1)}, bf16[256,512]{1,0:T(8,128)(2,1)S(1)}, bf16[256,512]{1,0:T(8,128)(2,1)S(1)}, f32[2,128]{1,0:T(2,128)S(1)}) custom-call(bf16[256,1024]{1,0:T(8,128)(2,1)S(1)} %copy-done, bf16[256,512]{1,0:T(8,128)(2,1)S(1)} %copy-done.2, bf16[256,512]{1,0:T(8,128)(2,1)S(1)} %copy-done.3, ...), custom_call_target="tpu_custom_call" | custom-call | tf_op jit(solution)/shard_map/pallas_call | solution.py:384
  64.0 0.5 slice_bitcast_fusion
  64.6 0.8 %copy.14 = bf16[256,1024]{1,0:T(8,128)(2,1)} copy(bf16[256,1024]{1,0:T(8,128)(2,1)S(1)} %get-tuple-element.20) | data formatting | bytes 1048576
  65.3 0.7 %copy.15 = bf16[256,512]{1,0:T(8,128)(2,1)} copy(bf16[256,512]{1,0:T(8,128)(2,1)S(1)} %get-tuple-element.21) | data formatting | bytes 524288
  66.1 0.7 %copy.16 = bf16[256,512]{1,0:T(8,128)(2,1)} copy(bf16[256,512]{1,0:T(8,128)(2,1)S(1)} %get-tuple-element.22) | data formatting | bytes 524288
Async XLA Ops:
  0.6 0.7 copy-start.4
  0.6 0.7 copy-start.5
  1.3 1.0 %copy-start = (bf16[256,1024]{1,0:T(8,128)(2,1)S(1)}, bf16[256,1024]{1,0:T(8,128)(2,1)}, u32[]{:S(2)}) copy-start(bf16[256,1024]{1,0:T(8,128)(2,1)} %q_in.1) | copy-start | bytes 1572868
  2.3 1.0 %copy-start.1 = (bf16[256,1024]{1,0:T(8,128)(2,1)S(1)}, bf16[256,1024]{1,0:T(8,128)(2,1)}, u32[]{:S(2)}) copy-start(bf16[256,1024]{1,0:T(8,128)(2,1)} %g_in.1) | copy-start | bytes 1572868
  3.4 0.9 %copy-start.2 = (bf16[256,512]{1,0:T(8,128)(2,1)S(1)}, bf16[256,512]{1,0:T(8,128)(2,1)}, u32[]{:S(2)}) copy-start(bf16[256,512]{1,0:T(8,128)(2,1)} %k_in.1) | copy-start | bytes 786436
  4.3 0.9 %copy-start.3 = (bf16[256,512]{1,0:T(8,128)(2,1)S(1)}, bf16[256,512]{1,0:T(8,128)(2,1)}, u32[]{:S(2)}) copy-start(bf16[256,512]{1,0:T(8,128)(2,1)} %v_in.1) | copy-start | bytes 786436

commit v3 on v2

--- a/solution.py
+++ b/solution.py
@@ -129,6 +129,7 @@
     for far, near in keys_in[1]:
         near.wait()
     fill(1, x, mine)
+    start_own(1, x)
     gain_acc[...] = jnp.zeros_like(gain_acc)
     for far, near in keys_in[0]:
         far.wait_recv()
@@ -143,7 +144,6 @@
     fill(1, 1 - x, theirs)
     forward(0, x)
     forward(0, 1 - x)
-    start_own(1, x)
     start_own(1, 1 - x)
     acc[...] = jnp.zeros_like(acc)
 
@@ -187,6 +187,13 @@
             delta_b[...] += jnp.sum(e * dp, axis=0, keepdims=True)
 
         for i in reversed(range(BLOCKS)):
+            if i == 1:
+                for g in range(2):
+                    @pl.when((s == 2 * g) & has_prev2)
+                    def _():
+                        send_on(g, 0).wait_recv()
+                        send_on(g, 1).wait_recv()
+
             keyed(i, first)
         il = 1.0 / l_b[...]
         delta = delta_b[...] * il
@@ -265,8 +272,7 @@
             acc[h, :, here, :] += got[h, 1, half].astype(F32)
 
         raw = k_b[rows, h * D : (h + 1) * D].astype(F32)
-        dk_raw, gain_part = norm_back(raw, inverse_norm(raw), kg[...], acc[h, 0, here, :])
-        gain_acc[1:2, :] += gain_part
+        dk_raw, _ = norm_back(raw, inverse_norm(raw), kg[...], acc[h, 0, here, :])
         dk_s[h, rows] = dk_raw.astype(BF16)
         dv_s[h, rows] = acc[h, 1, here, :].astype(BF16)
 
@@ -281,11 +287,6 @@
                 copy.start()
 
     def arrived(h):
-        @pl.when(has_prev2)
-        def _():
-            send_on(h, 0).wait_recv()
-            send_on(h, 1).wait_recv()
-
         for far, near in rows_in[h]:
             near.wait()
             far.wait_recv()
@@ -325,11 +326,15 @@
     lax.fori_loop(0, 4, step, 0)
     start_two(1, 1)
     start_one(1, 0)
-    finish(0, 0)
-    finish(0, 1)
-    start_one(1, 1)
-    finish(1, 0)
-    finish(1, 1)
+
+    def key_gain(hop):
+        rows = slice((4 - 2 * hop) * T, (6 - 2 * hop) * T)
+        for h in range(2):
+            gain_acc[1:2, :] += jnp.sum(acc[h, 0, rows, :] * kv[h, 0, rows, :].astype(F32), axis=0, keepdims=True)
+
+    key_gain(0)
+    pl.when(has_prev)(lambda: key_gain(1))
+    pl.when(has_prev2)(lambda: key_gain(2))
 
     def spread(size, me, axis, buf, snd, rcv):
         copies = []
@@ -337,19 +342,26 @@
             copies.append(remote(buf.at[me], buf.at[me], snd.at[k], rcv.at[k], {axis: lax.rem(me + k, size)}))
         for copy in copies:
             copy.start()
-        for copy in copies:
-            copy.wait_recv()
         return copies
 
     gain_c[c] = gain_acc[...]
-    sent = spread(n, c, "ctx", gain_c, c_snd, c_rcv)
+    over_ctx = spread(n, c, "ctx", gain_c, c_snd, c_rcv)
+    finish(0, 0)
+    finish(0, 1)
+    start_one(1, 1)
+    for copy in over_ctx:
+        copy.wait_recv()
     gain_t[tp] = jnp.sum(gain_c[...], axis=0)
-    sent += spread(m, tp, "tp", gain_t, t_snd, t_rcv)
+    over_tp = spread(m, tp, "tp", gain_t, t_snd, t_rcv)
+    finish(1, 0)
+    finish(1, 1)
+    for copy in over_tp:
+        copy.wait_recv()
     total = jnp.sum(gain_t[...], axis=0)
     gain_o[0:1, :] = total[0:1] * ((n * T * Q_HEADS) ** -0.5)
-    gain_o[1:2, :] = total[1:2] * ((n * T * KV_HEADS) ** -0.5)
-
-    for copy in sent:
+    gain_o[1:2, :] = total[1:2] / kg[...] * ((n * T * KV_HEADS) ** -0.5)
+
+    for copy in over_ctx + over_tp:
         copy.wait_send()
     for h in range(2):
         for far, _ in keys_in[h] + rows_in[h]:
@@ -418,7 +430,7 @@
             dma((n,)), dma((n,)), dma((m,)), dma((m,)),
         ],
         compiler_params=pltpu.CompilerParams(
-            collective_id=0, has_side_effects=True, vmem_limit_bytes=48 * 1024 * 1024
+            collective_id=0, has_side_effects=True, vmem_limit_bytes=63 * 1024 * 1024
         ),
     )(q_raw, k_raw, v_cur, d_out, q_gain.reshape(1, D), k_gain.reshape(1, D))
     return (dq_raw, dk_raw, dv, gains[0], gains[1])

time: 67 us -> 61.9 us (0.924)
  Pallas kernels: 58.7 us -> 56.1 us
  local copies, waits for them, and re-layouts: 7.35 us -> 4.84 us
    pallas_call x1, Pallas kernels: 58.7 us -> 56.1 us  [per_device(): pl.pallas_call(functools.partial(kernel, n, m), out_shape=(jax.ShapeDtype...]
    unnamed x15 -> x9, local copies, waits for them, and re-layouts: 6.83 us -> 4.32 us
where the time goes in v3:
time: 61.9 us; the launch traced here: 61.6 us
  Pallas kernels  56.1 us (91%)
  local copies, waits for them, and re-layouts  4.84 us (8%)
  between operations  0.65 us (1%)
    pallas_call x1, Pallas kernels, per_device(): pl.pallas_call(functools.partial(kernel, n, m), out_shape=(jax.ShapeDtype...  56.1 us
    unnamed x9, local copies, waits for them, and re-layouts  4.32 us

profile of v3, /device:TPU:0, one launch (start us, length us, event | category | flops | bytes accessed | tf_op | source)
XLA Modules:
  0.0 61.6 jit_solution(14854108054222667679)
XLA Ops:
  0.6 56.1 %shard_map.101 = (bf16[256,1024]{1,0:T(8,128)(2,1)}, bf16[256,512]{1,0:T(8,128)(2,1)}, bf16[256,512]{1,0:T(8,128)(2,1)}, f32[2,128]{1,0:T(2,128)}) custom-call(bf16[256,1024]{1,0:T(8,128)(2,1)} %q_in.1, bf16[256,512]{1,0:T(8,128)(2,1)} %k_in.1, bf16[256,512]{1,0:T(8,128)(2,1)} %v_in.1, bf16[256,1024]{1,0:T(8,128)(2,1)} %g_in.1, f32[1,128]{1,0:T(1,128)} %bitcast.6, ...), custom_call_target="tpu_custom_call" | custom-call | tf_op jit(solution)/shard_map/pallas_call | solution.py:396
  56.7 0.0 copy-start.2
  56.8 0.7 %copy-done.2 = f32[2,128]{1,0:T(2,128)S(1)} copy-done((f32[2,128]{1,0:T(2,128)S(1)}, f32[2,128]{1,0:T(2,128)}, u32[]{:S(2)}) %copy-start.2) | copy-done | bytes 1048
  57.4 0.5 slice_bitcast_fusion
  57.9 0.0 copy-start.1
  57.9 1.9 %copy.14 = bf16[256,1024]{1,0:T(8,128)(2,1)} copy(bf16[256,1024]{1,0:T(8,128)(2,1)} %get-tuple-element.20) | data formatting | bytes 1048576
  59.8 0.0 copy-done.1
  59.8 0.0 copy-start
  59.8 0.7 %copy.15 = bf16[256,512]{1,0:T(8,128)(2,1)} copy(bf16[256,512]{1,0:T(8,128)(2,1)S(1)} %copy-done.1) | data formatting | bytes 524288
  60.6 0.3 copy-done
  60.9 0.7 %copy.16 = bf16[256,512]{1,0:T(8,128)(2,1)} copy(bf16[256,512]{1,0:T(8,128)(2,1)S(1)} %copy-done) | data formatting | bytes 524288
Async XLA Ops:
  56.7 0.7 %copy-start.2 = (f32[2,128]{1,0:T(2,128)S(1)}, f32[2,128]{1,0:T(2,128)}, u32[]{:S(2)}) copy-start(f32[2,128]{1,0:T(2,128)} %get-tuple-element.12) | copy-start | bytes 3076
  57.9 1.9 %copy-start.1 = (bf16[256,512]{1,0:T(8,128)(2,1)S(1)}, bf16[256,512]{1,0:T(8,128)(2,1)}, u32[]{:S(2)}) copy-start(bf16[256,512]{1,0:T(8,128)(2,1)} %get-tuple-element.21) | copy-start | bytes 786436
  59.8 1.0 %copy-start = (bf16[256,512]{1,0:T(8,128)(2,1)S(1)}, bf16[256,512]{1,0:T(8,128)(2,1)}, u32[]{:S(2)}) copy-start(bf16[256,512]{1,0:T(8,128)(2,1)} %get-tuple-element.22) | copy-start | bytes 786436

commit v4 on v3

--- a/solution.py
+++ b/solution.py
@@ -137,13 +137,15 @@
     start_own(0, 1 - x)
     for far, near in keys_in[1]:
         far.wait_recv()
-    for h in range(2):
-        for far, near in rows_in[h]:
-            near.start()
-            far.start()
+    for far, near in rows_in[0]:
+        near.start()
+        far.start()
     fill(1, 1 - x, theirs)
     forward(0, x)
     forward(0, 1 - x)
+    for far, near in rows_in[1]:
+        near.start()
+        far.start()
     start_own(1, 1 - x)
     acc[...] = jnp.zeros_like(acc)
 
@@ -173,6 +175,17 @@
                 def _():
                     body(i, pl.ds(start, T))
 
+        def each(which, body):
+            @pl.when(has_prev2)
+            def _():
+                for i in which:
+                    body(i, pl.ds(pl.multiple_of((qb + i) * T, T), T))
+
+            @pl.when(jnp.logical_not(has_prev2))
+            def _():
+                for i in which:
+                    keyed(i, body)
+
         def first(i, keys):
             scores = nt(kv[h, 0, keys, :], queries)
             e = jnp.exp(scores * score_scale)
@@ -186,15 +199,14 @@
             l_b[...] += jnp.sum(e, axis=0, keepdims=True)
             delta_b[...] += jnp.sum(e * dp, axis=0, keepdims=True)
 
-        for i in reversed(range(BLOCKS)):
-            if i == 1:
-                for g in range(2):
-                    @pl.when((s == 2 * g) & has_prev2)
-                    def _():
-                        send_on(g, 0).wait_recv()
-                        send_on(g, 1).wait_recv()
-
-            keyed(i, first)
+        each((4, 3, 2), first)
+        for g in range(2):
+            @pl.when((s == 2 * g) & has_prev2)
+            def _():
+                send_on(g, 0).wait_recv()
+                send_on(g, 1).wait_recv()
+
+        each((1, 0), first)
         il = 1.0 / l_b[...]
         delta = delta_b[...] * il
 
@@ -205,8 +217,7 @@
             acc[h, 1, keys, :] += jnp.dot(p.astype(BF16), grads, preferred_element_type=F32)
             dqt[...] += tn(kv[h, 0, keys, :], ds)
 
-        for i in range(BLOCKS):
-            keyed(i, second)
+        each(range(BLOCKS), second)
         dq = jnp.transpose(dqt[...])
         dq_raw, gain_part = norm_back(raw, inv, qg[...], dq)
         gain_acc[0:1, :] += gain_part

time: 61.9 us -> 61.2 us (0.989)
    pallas_call x1, Pallas kernels: 56.1 us -> 55.5 us  [per_device(): pl.pallas_call(functools.partial(kernel, n, m), out_shape=(jax.ShapeDtype...]
where the time goes in v4:
time: 61.2 us; the launch traced here: 61 us
  Pallas kernels  55.5 us (91%)
  local copies, waits for them, and re-layouts  4.84 us (8%)
  between operations  0.65 us (1%)
    pallas_call x1, Pallas kernels, per_device(): pl.pallas_call(functools.partial(kernel, n, m), out_shape=(jax.ShapeDtype...  55.5 us
    unnamed x9, local copies, waits for them, and re-layouts  4.32 us

profile of v4, /device:TPU:0, one launch (start us, length us, event | category | flops | bytes accessed | tf_op | source)
XLA Modules:
  0.0 61.0 jit_solution(2192539528533877318)
XLA Ops:
  0.6 55.5 %shard_map.101 = (bf16[256,1024]{1,0:T(8,128)(2,1)}, bf16[256,512]{1,0:T(8,128)(2,1)}, bf16[256,512]{1,0:T(8,128)(2,1)}, f32[2,128]{1,0:T(2,128)}) custom-call(bf16[256,1024]{1,0:T(8,128)(2,1)} %q_in.1, bf16[256,512]{1,0:T(8,128)(2,1)} %k_in.1, bf16[256,512]{1,0:T(8,128)(2,1)} %v_in.1, bf16[256,1024]{1,0:T(8,128)(2,1)} %g_in.1, f32[1,128]{1,0:T(1,128)} %bitcast.6, ...), custom_call_target="tpu_custom_call" | custom-call | tf_op jit(solution)/shard_map/pallas_call | solution.py:407
  56.1 0.0 copy-start.2
  56.1 0.7 %copy-done.2 = f32[2,128]{1,0:T(2,128)S(1)} copy-done((f32[2,128]{1,0:T(2,128)S(1)}, f32[2,128]{1,0:T(2,128)}, u32[]{:S(2)}) %copy-start.2) | copy-done | bytes 1048
  56.8 0.5 slice_bitcast_fusion
  57.3 0.0 copy-start.1
  57.3 1.9 %copy.14 = bf16[256,1024]{1,0:T(8,128)(2,1)} copy(bf16[256,1024]{1,0:T(8,128)(2,1)} %get-tuple-element.20) | data formatting | bytes 1048576
  59.2 0.0 copy-done.1
  59.2 0.0 copy-start
  59.2 0.7 %copy.15 = bf16[256,512]{1,0:T(8,128)(2,1)} copy(bf16[256,512]{1,0:T(8,128)(2,1)S(1)} %copy-done.1) | data formatting | bytes 524288
  59.9 0.3 copy-done
  60.3 0.7 %copy.16 = bf16[256,512]{1,0:T(8,128)(2,1)} copy(bf16[256,512]{1,0:T(8,128)(2,1)S(1)} %copy-done) | data formatting | bytes 524288
Async XLA Ops:
  56.1 0.7 %copy-start.2 = (f32[2,128]{1,0:T(2,128)S(1)}, f32[2,128]{1,0:T(2,128)}, u32[]{:S(2)}) copy-start(f32[2,128]{1,0:T(2,128)} %get-tuple-element.12) | copy-start | bytes 3076
  57.3 1.9 %copy-start.1 = (bf16[256,512]{1,0:T(8,128)(2,1)S(1)}, bf16[256,512]{1,0:T(8,128)(2,1)}, u32[]{:S(2)}) copy-start(bf16[256,512]{1,0:T(8,128)(2,1)} %get-tuple-element.21) | copy-start | bytes 786436
  59.2 1.0 %copy-start = (bf16[256,512]{1,0:T(8,128)(2,1)S(1)}, bf16[256,512]{1,0:T(8,128)(2,1)}, u32[]{:S(2)}) copy-start(bf16[256,512]{1,0:T(8,128)(2,1)} %get-tuple-element.22) | copy-start | bytes 786436
